TPU v7x, 128 devices: a whole 4x4x4 slice. The times are simulated.
128 devices in a mesh: dom: 32 (over z, x, core), blk: 4 (over y).
Axes of the slice: x: 4, y: 4, z: 4, core: 2. Of those that a mesh axis runs over, the one named last changes fastest.
Arguments:
- displacement: float32 [16384, 96], P(('dom', 'blk')), may hold values from -6 to 6
- damage: float32 [16384, 96], P(('dom', 'blk')), may hold values from 0 to 0.95
- applied_load: float32 [16384, 96], P(('dom', 'blk')), may hold values from -300 to 300
- tangent: bfloat16 [16384, 5, 96, 96], P(('dom', 'blk')), may hold values from -0.625 to 0.625
- laplacian: bfloat16 [16384, 5, 96, 96], P(('dom', 'blk')), may hold values from -0.25 to 0.25
- block_columns: int32 [16384, 5], P(('dom', 'blk')), may hold values from 0 to 1023, as said below
- send_lists: int32 [32, 2, 256], P('dom'), may hold values from -1 to 511, as said below
- hist_mech: float32 [16384, 27, 96], P(('dom', 'blk')), may hold values from 0 to 200
- mech_dest: int32 [16384], P(('dom', 'blk')), may hold values from 0 to 16383, as said below
- strain_matrix: float32 [27, 96, 96], replicated, may hold values from -0.625 to 0.625
- quad_weight: float32 [27], replicated, may hold values from 0.018518519 to 0.055555556
Outputs:
- mech_out: float32 [16384, 96], P(('dom', 'blk'))
- dmg_out: float32 [16384, 96], P(('dom', 'blk'))
- norms: float32 [2], replicated
Inputs may be any that keep to these rules, and one draw needn't show every extreme that they name: mech_dest is a permutation of the block rows. The 128 rows of one device go to at most 2 rows of any one device (itself included), and that many are reached in every draw. `send_lists`: -1 marks an unused slot; used slots come first and name distinct rows of the group, numbered within the group. Group 0 lists nothing for the group below and the last group nothing for the group above. Some list uses all 256 slots. `block_columns`: entries of the ghost parts of the extended numbering name only used slots of the neighbours' lists, never those of a missing neighbour, and every used slot is named by some block row of the receiving group.
All inputs are finite; a program needn't handle non-finite values.
Results may differ from a plain program's by a relative error of at most 0.00047.
Values may be sent and summed in bfloat16 or wider, within the bound.
A program may use at most 128 MiB of HBM per device.

v0:
```python
import jax
import jax.numpy as jnp
from jax import lax
from jax.sharding import PartitionSpec as P


def padded(x, sides, width):
    for axis, dim in sides:
        peers, length = (lax.axis_size(axis), x.shape[dim])
        up = [(i, (i + 1) % peers) for i in range(peers - 1)]
        down = [(j, i) for i, j in up]
        last = lax.slice_in_dim(x, length - width, length, axis=dim)
        leading = lax.slice_in_dim(x, 0, width, axis=dim)
        before = lax.ppermute(last, axis, up)
        after = lax.ppermute(leading, axis, down)
        x = jnp.concatenate([before, x, after], axis=dim)
    return x


def on_device(
    displacement,
    damage,
    applied_load,
    tangent,
    laplacian,
    block_columns,
    send_lists,
    hist_mech,
    mech_dest,
    strain_matrix,
    quad_weight,
):
    row_count = displacement.shape[0]
    width = displacement.shape[1]
    devices = lax.axis_size(("dom", "blk"))
    capacity = row_count // devices + 1
    root_deg = jnp.sqrt((1.0 - damage) ** 2 + 0.001)
    fields = jnp.stack(
        [(root_deg * displacement).astype(jnp.bfloat16), damage.astype(jnp.bfloat16)]
    )
    group_fields = lax.all_gather(fields, "blk", axis=1, tiled=True)
    own_lists = send_lists[0]
    safe_index = jnp.maximum(own_lists, 0)
    picked = group_fields[:, safe_index]
    picked = jnp.where((own_lists >= 0)[None, :, :, None], picked, jnp.zeros((), jnp.bfloat16))
    framed = padded(picked, (("dom", 1),), 1)
    lower_ghost = framed[:, 0]
    upper_ghost = framed[:, 3]
    extended = jnp.concatenate([group_fields, lower_ghost, upper_ghost], axis=1)
    near_rows = extended[:, block_columns]
    mech_sum = jnp.einsum("ikrc,ikc->ir", tangent, near_rows[0], preferred_element_type=jnp.float32)
    diffuse = jnp.einsum(
        "ikrc,ikc->ir", laplacian, near_rows[1], preferred_element_type=jnp.float32
    )
    mech_res = root_deg * mech_sum - applied_load
    dest_device = mech_dest // row_count
    dest_slot = mech_dest % row_count
    dest_marks = (dest_device[:, None] == jnp.arange(devices, dtype=jnp.int32)[None, :]).astype(
        jnp.int32
    )
    slot_rank = jnp.sum(jnp.cumsum(dest_marks, axis=0) * dest_marks, axis=1) - 1
    bucket = dest_device * capacity + slot_rank
    slot_table = (
        jnp.full((devices * capacity,), -1, jnp.int32)
        .at[bucket]
        .set(dest_slot)
        .reshape(devices, capacity)
    )
    parcel = (
        jnp.zeros((devices * capacity,) + hist_mech.shape[1:], jnp.float32)
        .at[bucket]
        .set(hist_mech)
    )
    parcel = parcel.reshape((devices, capacity) + hist_mech.shape[1:])
    got_slots, got_rows = (
        lax.all_to_all(slot_table, ("dom", "blk"), split_axis=0, concat_axis=0, tiled=True),
        lax.all_to_all(parcel, ("dom", "blk"), split_axis=0, concat_axis=0, tiled=True),
    )
    target = jnp.where(got_slots >= 0, got_slots, row_count).reshape(-1)
    history = (
        jnp.zeros_like(hist_mech)
        .at[target]
        .set(got_rows.reshape((-1,) + hist_mech.shape[1:]), mode="drop")
    )
    strain = jnp.einsum("qcr,ir->iqc", strain_matrix, displacement, precision=lax.Precision.HIGHEST)
    energy = 0.5 * strain * strain
    source = jnp.einsum(
        "q,iqc->ic", quad_weight, jnp.maximum(history, energy), precision=lax.Precision.HIGHEST
    )
    dmg_res = diffuse + (1.0 + 2.0 * source) * damage - 2.0 * source
    totals = lax.psum((jnp.sum(mech_res * mech_res), jnp.sum(dmg_res * dmg_res)), ("dom", "blk"))
    entries = row_count * width * devices
    mech_norm = jnp.sqrt(totals[0] / entries + 1e-06)
    dmg_norm = jnp.sqrt(totals[1] / entries + 1e-06)
    return (mech_res / mech_norm, dmg_res / dmg_norm, jnp.stack([mech_norm, dmg_norm]))


def solution(mesh):
    in_specs = (
        P(("dom", "blk"), None),
        P(("dom", "blk"), None),
        P(("dom", "blk"), None),
        P(("dom", "blk"), None, None, None),
        P(("dom", "blk"), None, None, None),
        P(("dom", "blk"), None),
        P("dom", None, None),
        P(("dom", "blk"), None, None),
        P(("dom", "blk")),
        P(),
        P(),
    )
    out_specs = (P(("dom", "blk"), None), P(("dom", "blk"), None), P())
    return jax.shard_map(
        on_device, mesh=mesh, in_specs=in_specs, out_specs=out_specs, check_vma=False
    )
```

profile of v0, /device:TPU:1, one launch (start us, length us, event | category | flops | bytes accessed | tf_op | source)
XLA Modules:
  0.0 223.9 jit_solution(6956331945346940331)
XLA Ops:
  0.7 0.8 maximum_bitcast_fusion
  1.5 0.7 compare_bitcast_fusion
  2.1 0.9 fusion.6
  3.1 11.1 %all_gather.3 = bf16[2,512,96]{1,2,0:T(8,128)(2,1)S(1)} all-gather(bf16[2,128,96]{1,2,0:T(8,128)(2,1)S(1)} %pad_maximum_fusion.1), channel_id=1, replica_groups=mesh['dom'=32,'blk'=4] {'blk'}, dimensions={1}, use_global_device_ids=true | all-gather | bytes 245760 | tf_op jit(solution)/shard_map/all_gather | solution.py:41
  14.3 2.1 gather_fusion
  16.4 1.1 fusion.3
  17.5 0.9 fusion.11
  18.5 4.2 %collective-permute-start.1 = (bf16[2,1,256,96]{3,0,2,1:T(2,128)(2,1)}, bf16[2,1,256,96]{3,0,2,1:T(2,128)(2,1)}, u32[]{:S(2)}, u32[]{:S(2)}) collective-permute-start(bf16[2,1,256,96]{3,0,2,1:T(2,128)(2,1)} %get-tuple-element.13), channel_id=1, source_target_pairs={{4,0},{8,4},{12,8},{16,12},{20,16},{24,20},{28,24},{32,28},{36,32}... | collective-permute-start | bytes 294920 | tf_op jit(solution)/shard_map/ppermute | solution.py:15
  22.7 3.0 %collective-permute-start = (bf16[2,1,256,96]{3,0,2,1:T(2,128)(2,1)}, bf16[2,1,256,96]{3,0,2,1:T(2,128)(2,1)}, u32[]{:S(2)}, u32[]{:S(2)}) collective-permute-start(bf16[2,1,256,96]{3,0,2,1:T(2,128)(2,1)} %get-tuple-element.12), channel_id=1, source_target_pairs={{0,4},{4,8},{8,12},{12,16},{16,20},{20,24},{24,28},{28,32},{32,36}... | collective-permute-start | bytes 294920 | tf_op jit(solution)/shard_map/ppermute | solution.py:14
  26.2 1.0 scatter_custom_fusion
  27.2 0.8 all_to_all.11
  27.9 9.0 %all-to-all-start = ((s32[128,1,2]{2,1,0:T(1,128)}), s32[128,1,2]{2,1,0:T(1,128)S(1)}, u32[]{:S(2)}, u32[]{:S(2)}) async-start(s32[128,1,2]{2,1,0:T(1,128)} %bitcast.20), calls=%async_computation | async-start | bytes 131072 | tf_op jit(solution)/shard_map/all_to_all | solution.py:76
  37.2 2.3 %copy.47 = f32[128,27,96]{2,1,0:T(8,128)S(1)} copy(f32[128,27,96]{0,2,1:T(8,128)} %param.18) | data formatting | bytes 2654208 | tf_op args[7]
  39.5 2.5 %broadcast_in_dim.44 = f32[256,27,96]{2,1,0:T(8,128)} broadcast(f32[]{:T(128)} %constant.30.clone.1), dimensions={} | broadcast | bytes 2654212 | tf_op jit(solution)/shard_map/broadcast_in_dim | solution.py:70
  42.0 15.7 %scatter_fusion = f32[256,27,96]{2,1,0:T(8,128)} fusion(f32[256,27,96]{2,1,0:T(8,128)} %broadcast_in_dim.44, s32[128]{0:T(128)S(1)} %compare_select_fusion.3, f32[128,27,96]{2,1,0:T(8,128)S(1)} %copy.47), kind=kCustom, calls=%fused_computation.3 | custom fusion | bytes 3981824 | tf_op jit(solution)/shard_map/scatter | solution.py:72
  57.7 7.4 %copy.49 = f32[128,2,27,96]{3,1,2,0:T(2,128)} copy(f32[128,2,27,96]{3,2,1,0:T(8,128)} %bitcast.49) | data formatting | bytes 5308416 | tf_op jit(solution)/shard_map/reshape | solution.py:74
  65.1 10.2 %all-to-all-start.1 = ((f32[128,2,27,96]{3,1,2,0:T(2,128)}), f32[128,2,27,96]{3,1,2,0:T(2,128)}, u32[]{:S(2)}, u32[]{:S(2)}) async-start(f32[128,2,27,96]{3,1,2,0:T(2,128)} %copy.49), calls=%async_computation.1 | async-start | bytes 7077888 | tf_op jit(solution)/shard_map/all_to_all | solution.py:77
  75.8 0.8 reduce.7
  76.8 1.8 pad_maximum_fusion
  78.7 2.8 %gather_fusion.1 = bf16[640,2,96]{2,1,0:T(2,128)(2,1)S(1)} fusion(bf16[2,1024,96]{2,0,1:T(2,128)(2,1)S(1)} %pad_maximum_fusion, s32[1024]{0:T(1024)S(1)} %pad_clamp_fusion), kind=kCustom, calls=%fused_computation.1 | custom fusion | bytes 494080 | tf_op jit(solution)/shard_map/gather | solution.py:50
  82.4 11.1 %multiply_reduce_fusion = (f32[128,96]{0,1:T(8,128)S(1)}, f32[128,96]{0,1:T(8,128)S(1)}) fusion(f32[128,96,5]{0,1,2:T(8,128)S(1)} %bitcast_convert_fusion, bf16[128,5,96,96]{0,3,2,1:T(8,128)(2,1)} %param.15, bf16[128,5,96,96]{0,3,2,1:T(8,128)(2,1)} %param.14, f32[128,96,5]{0,1,2:T(8,128)S(1)} %bitcast_convert_fusion.1), kind=kLoop, calls=%fused_computation.5 | loop fusion | flops 35364864 | bytes 24182784 | tf_op jit(solution)/shard_map/ikrc,ikc->ir/dot_general | solution.py:52
  93.5 27.7 %all-to-all-done.1 = f32[128,2,27,96]{3,1,2,0:T(2,128)} async-done(((f32[128,2,27,96]{3,1,2,0:T(2,128)}), f32[128,2,27,96]{3,1,2,0:T(2,128)}, u32[]{:S(2)}, u32[]{:S(2)}) %all-to-all-start.1) | async-done | bytes 2654240 | tf_op jit(solution)/shard_map/all_to_all | solution.py:77
  121.2 3.9 %copy.50 = f32[128,2,27,96]{3,1,0,2:T(2,128)S(1)} copy(f32[128,2,27,96]{3,1,2,0:T(2,128)} %all-to-all-done.1) | data formatting | bytes 5308416 | tf_op jit(solution)/shard_map/all_to_all | solution.py:77
  125.1 4.0 %copy.51 = f32[256,27,96]{2,1,0:T(8,128)} copy(f32[256,27,96]{2,0,1:T(8,128)S(1)} %bitcast.50) | data formatting | bytes 5308416 | tf_op jit(solution)/shard_map/reshape | solution.py:83
  129.4 22.2 %scatter_fusion.1 = f32[128,27,96]{2,1,0:T(8,128)S(1)} fusion(f32[128,27,96]{2,1,0:T(8,128)S(1)} %broadcast_in_dim.40, s32[256]{0:T(256)S(1)} %bitcast.56, f32[256,27,96]{2,1,0:T(8,128)} %copy.51), kind=kCustom, calls=%fused_computation.4 | custom fusion | bytes 7963648 | tf_op jit(solution)/shard_map/scatter | solution.py:83
  151.7 1.8 copy.52
  153.4 2.6 %fusion.2 = f32[128,27,96]{0,2,1:T(8,128)S(1)} fusion(f32[128,27,96]{0,2,1:T(8,128)} %copy.52, f32[27,96,96]{2,1,0:T(8,128)S(1)} %copy-done, f32[128,96]{0,1:T(8,128)} %param.11), kind=kOutput, calls=%fused_computation.10 | convolution fusion | flops 383201280 | bytes 3698688 | tf_op jit(solution)/shard_map/qcr,ir->iqc/dot_general | solution.py:85
  156.0 1.8 fusion
  157.9 0.6 multiply_reduce_fusion.2
  158.5 62.7 %all-reduce = (f32[]{:T(128)}, f32[]{:T(128)}) all-reduce(f32[]{:T(128)} %get-tuple-element.7, f32[]{:T(128)} %get-tuple-element.6), channel_id=1, replica_groups=mesh['dom'=32,'blk'=4] {'dom','blk'}, use_global_device_ids=true, to_apply=%region_1.2 | all-reduce | flops 2 | bytes 16 | tf_op jit(solution)/shard_map/psum | solution.py:91
  222.6 0.7 broadcast_divide_fusion
  223.3 0.6 pad_maximum_fusion.2
  (41 shorter events, 2.7 us)
Async XLA Ops:
  0.6 152.8 %copy-start = (f32[27,96,96]{2,1,0:T(8,128)S(1)}, f32[27,96,96]{2,1,0:T(8,128)}, u32[]{:S(2)}) copy-start(f32[27,96,96]{2,1,0:T(8,128)} %param.20) | copy-start | bytes 2985988
  0.6 25.1 %copy-start.7 = (s32[128]{0:T(128)S(1)}, s32[128]{0:T(128)}, u32[]{:S(2)}) copy-start(s32[128]{0:T(128)} %param.19) | copy-start | bytes 1540
  0.7 36.2 %copy-start.5 = (s32[128,5]{0,1:T(8,128)S(1)}, s32[128,5]{0,1:T(8,128)}, u32[]{:S(2)}) copy-start(s32[128,5]{0,1:T(8,128)} %param.16) | copy-start | bytes 7684
  14.3 22.9 %copy-start.1 = (bf16[2,512,96]{2,0,1:T(2,128)(2,1)}, bf16[2,512,96]{2,0,1:T(2,128)(2,1)S(1)}, u32[]{:S(2)}) copy-start(bf16[2,512,96]{2,0,1:T(2,128)(2,1)S(1)} %copy.42) | copy-start | bytes 589828
  18.5 58.3 %collective-permute-start.1 = (bf16[2,1,256,96]{3,0,2,1:T(2,128)(2,1)}, bf16[2,1,256,96]{3,0,2,1:T(2,128)(2,1)}, u32[]{:S(2)}, u32[]{:S(2)}) collective-permute-start(bf16[2,1,256,96]{3,0,2,1:T(2,128)(2,1)} %get-tuple-element.13), channel_id=1, source_target_pairs={{4,0},{8,4},{12,8},{16,12},{20,16},{24,20},{28,24},{32,28},{36,32}... | collective-permute-start | bytes 294920 | tf_op jit(solution)/shard_map/ppermute | solution.py:15
  22.7 54.1 %collective-permute-start = (bf16[2,1,256,96]{3,0,2,1:T(2,128)(2,1)}, bf16[2,1,256,96]{3,0,2,1:T(2,128)(2,1)}, u32[]{:S(2)}, u32[]{:S(2)}) collective-permute-start(bf16[2,1,256,96]{3,0,2,1:T(2,128)(2,1)} %get-tuple-element.12), channel_id=1, source_target_pairs={{0,4},{4,8},{8,12},{12,16},{16,20},{20,24},{24,28},{28,32},{32,36}... | collective-permute-start | bytes 294920 | tf_op jit(solution)/shard_map/ppermute | solution.py:14
  27.9 37.2 %all-to-all-start = ((s32[128,1,2]{2,1,0:T(1,128)}), s32[128,1,2]{2,1,0:T(1,128)S(1)}, u32[]{:S(2)}, u32[]{:S(2)}) async-start(s32[128,1,2]{2,1,0:T(1,128)} %bitcast.20), calls=%async_computation | async-start | bytes 131072 | tf_op jit(solution)/shard_map/all_to_all | solution.py:76
  65.1 11.7 %copy-start.2 = (bf16[2,512,96]{2,0,1:T(2,128)(2,1)S(1)}, bf16[2,512,96]{2,0,1:T(2,128)(2,1)}, u32[]{:S(2)}) copy-start(bf16[2,512,96]{2,0,1:T(2,128)(2,1)} %copy-done.1) | copy-start | bytes 589828
  65.1 56.1 %all-to-all-start.1 = ((f32[128,2,27,96]{3,1,2,0:T(2,128)}), f32[128,2,27,96]{3,1,2,0:T(2,128)}, u32[]{:S(2)}, u32[]{:S(2)}) async-start(f32[128,2,27,96]{3,1,2,0:T(2,128)} %copy.49), calls=%async_computation.1 | async-start | bytes 7077888 | tf_op jit(solution)/shard_map/all_to_all | solution.py:77
  153.4 2.6 %copy-start.6 = (f32[27]{0:T(128)S(1)}, f32[27]{0:T(128)}, u32[]{:S(2)}) copy-start(f32[27]{0:T(128)} %param.21) | copy-start | bytes 328
  153.4 4.4 %copy-start.3 = (f32[128,96]{0,1:T(8,128)S(1)}, f32[128,96]{0,1:T(8,128)}, u32[]{:S(2)}) copy-start(f32[128,96]{0,1:T(8,128)} %param.12) | copy-start | bytes 147460
  153.4 4.4 %copy-start.4 = (f32[128,96]{0,1:T(8,128)S(1)}, f32[128,96]{0,1:T(8,128)}, u32[]{:S(2)}) copy-start(f32[128,96]{0,1:T(8,128)} %param.13) | copy-start | bytes 147460
where the time goes:
time: 225 us; the launch traced here: 224 us
  blocking collectives  73.8 us (33%)
  local copies, waits for them, and re-layouts  69.6 us (31%)
  waiting for transfers between devices  27.7 us (12%)
  starting transfers between devices  26.3 us (12%)
  other arithmetic  19.6 us (9%)
  matrix products  4.4 us (2%)
  between operations  2.38 us (1%)
    psum x1, blocking collectives, on_device(): lax.psum((jnp.sum(mech_res * mech_res), jnp.sum(dmg_res * dmg_res)), ('do...  62.7 us
    all_to_all x1, waiting for transfers between devices, on_device(): lax.all_to_all(parcel, ('dom', 'blk'), split_axis=0, concat_axis=0, tiled...  27.7 us
    scatter x2, local copies, waits for them, and re-layouts, on_device(): history = jnp.zeros_like(hist_mech).at[target].set(got_rows.reshape((-1,)...  24 us
    scatter x1, local copies, waits for them, and re-layouts, on_device(): parcel = jnp.zeros((devices * capacity,) + hist_mech.shape[1:], jnp.float...  15.7 us
    dot_general x1, other arithmetic, on_device(): jnp.einsum('ikrc,ikc->ir', laplacian, near_rows[1], preferred_element_typ...  11.1 us
    all_gather x1, blocking collectives, on_device(): group_fields = lax.all_gather(fields, 'blk', axis=1, tiled=True)  11.1 us
    all_to_all x1, starting transfers between devices, on_device(): lax.all_to_all(parcel, ('dom', 'blk'), split_axis=0, concat_axis=0, tiled...  10.2 us
    all_to_all x1, starting transfers between devices, on_device(): lax.all_to_all(slot_table, ('dom', 'blk'), split_axis=0, concat_axis=0, t...  8.96 us
  transfers between devices with their start and end apart: 4, of which 1 were waited for; matrix products, arithmetic and copies ran while one was open for 21% of the time, Pallas kernels for 0%

commit v1 on v0

v1 whole, which is shorter than its diff:
```python
import functools

import jax
import jax.numpy as jnp
from jax import lax
from jax.experimental import pallas as pl
from jax.experimental.pallas import tpu as pltpu
from jax.sharding import PartitionSpec as P

MESH = pl.DeviceIdType.MESH
F32 = jnp.float32
BF16 = jnp.bfloat16
LANES = 128


def dot(a, b):
    return jnp.dot(a, b, preferred_element_type=F32)


def dot_nt(a, b):
    return lax.dot_general(a, b, (((1,), (1,)), ((), ())), preferred_element_type=F32)


def halves(x):
    hi = x.astype(BF16)
    return hi, (x - hi.astype(F32)).astype(BF16)


def as_bf16(mask):
    return jnp.where(mask, 1.0, 0.0).astype(BF16)


def bytes_wait(ref, sem):
    pltpu.make_async_copy(ref, ref, sem).wait()


def block_rows(mat, near, out):
    kblk, width = near.shape[0], near.shape[1]

    def rows(rb, carry):
        r0 = pl.multiple_of(rb * 8, 8)
        acc = None
        for k in range(kblk):
            for c in range(0, width, 16):
                part = mat[k, pl.ds(r0, 8), c : c + 16, :].astype(F32) * near[k, c : c + 16, :][None]
                acc = part if acc is None else acc + part
        out[pl.ds(r0, 8), :] = jnp.sum(acc, axis=1)
        return carry

    lax.fori_loop(0, width // 8, rows, 0)


def kernel(
    nd,
    nb,
    disp_h,
    dmg_h,
    load_h,
    tan_h,
    lap_h,
    cols_h,
    lists_h,
    hist_h,
    dest_h,
    smat_h,
    quad_h,
    mech_o,
    dmg_o,
    norm_o,
    disp,
    dmg,
    load,
    tan,
    lap,
    cols,
    lists,
    hist,
    smat,
    quad,
    dall,
    grp_d,
    grp_w,
    pick_d,
    pick_w,
    ghost_d,
    ghost_w,
    pickhot,
    nearhot,
    near_d,
    near_w,
    s_hi,
    s_lo,
    diffuse,
    mech,
    ohm,
    h2s,
    h2r,
    h3s,
    h3r,
    ld,
    ss,
    rs,
):
    n = nd * nb
    g1 = 2 * nb
    g2 = n // g1
    width, rows = disp.shape
    kblk = cols.shape[0]
    gmax = lists.shape[1]
    shift = rows.bit_length() - 1
    wl = h2s.shape[2] // 2
    dom = lax.axis_index("dom")
    blk = lax.axis_index("blk")
    me = dom * nb + blk
    base = (me // g1) * g1

    def loc(p):
        return (p // nb, lax.rem(p, nb))

    def signal(p):
        pl.semaphore_signal(barrier, inc=1, device_id=loc(p), device_id_type=MESH)

    def send(src, dst, s, r, p):
        pltpu.make_async_remote_copy(
            src_ref=src, dst_ref=dst, send_sem=s, recv_sem=r, device_id=loc(p), device_id_type=MESH
        ).start()

    barrier = pltpu.get_barrier_semaphore()

    @pl.loop(1, g1)
    def _(j):
        signal(base + lax.rem(me + j, g1))

    @pl.loop(1, g2)
    def _(j):
        signal(lax.rem(me + g1 * j, n))

    signal(lax.rem(me + nb, n))
    signal(lax.rem(me + n - nb, n))

    loads = []
    for i, (src, dst) in enumerate(
        (
            (dmg_h, dmg),
            (disp_h, disp),
            (dest_h, dall.at[me]),
            (lists_h, lists),
            (cols_h, cols),
            (lap_h, lap),
            (smat_h, smat),
            (hist_h, hist),
            (tan_h, tan),
            (load_h, load),
            (quad_h, quad),
        )
    ):
        copy = pltpu.make_async_copy(src, dst, ld.at[i])
        copy.start()
        loads.append(copy)
    c_dmg, c_disp, c_dest, c_lists, c_cols, c_lap, c_smat, c_hist, c_tan, c_load, c_quad = loads

    c_dmg.wait()
    damage = dmg[...]
    grp_d[blk] = damage.astype(BF16)
    c_disp.wait()
    root = jnp.sqrt((1.0 - damage) ** 2 + 0.001)
    grp_w[blk] = (root * disp[...]).astype(BF16)
    c_dest.wait()
    pl.semaphore_wait(barrier, g1 + g2)

    @pl.loop(1, nb)
    def _(j):
        p = dom * nb + lax.rem(blk + j, nb)
        send(grp_d.at[blk], grp_d.at[blk], ss.at[0], rs.at[0], p)

    @pl.loop(1, g1)
    def _(j):
        send(dall.at[me], dall.at[me], ss.at[1], rs.at[1], base + lax.rem(me + j, g1))

    @pl.loop(1, nb)
    def _(j):
        p = dom * nb + lax.rem(blk + j, nb)
        send(grp_w.at[blk], grp_w.at[blk], ss.at[2], rs.at[2], p)

    c_lists.wait()
    for side in range(2):
        row = lax.broadcasted_iota(jnp.int32, (nb * rows, gmax), 0)
        pickhot[side] = as_bf16(row == lists[side : side + 1, :])

    bytes_wait(dall.at[pl.ds(0, g1 - 1)], rs.at[1])

    @pl.loop(1, g2)
    def _(j):
        part = dall.at[pl.ds(base, g1)]
        send(part, part, ss.at[3], rs.at[3], lax.rem(me + g1 * j, n))

    def pick(grp, out, ghost, at):
        for side in range(2):
            total = None
            for b in range(nb):
                part = dot(grp[b], pickhot[side, b * rows : (b + 1) * rows, :])
                total = part if total is None else total + part
            out[side] = total.astype(BF16)

        @pl.when(dom > 0)
        def _():
            send(out.at[0], ghost.at[1], ss.at[at], rs.at[at + 1], me - nb)

        @pl.when(dom < nd - 1)
        def _():
            send(out.at[1], ghost.at[0], ss.at[at + 1], rs.at[at], me + nb)

    bytes_wait(grp_d.at[pl.ds(0, nb - 1)], rs.at[0])
    pick(grp_d, pick_d, ghost_d, 4)
    bytes_wait(grp_w.at[pl.ds(0, nb - 1)], rs.at[2])
    pick(grp_w, pick_w, ghost_w, 6)

    c_cols.wait()
    for k in range(kblk):
        entry = lax.broadcasted_iota(jnp.int32, (nearhot.shape[0], rows), 0)
        nearhot[:, k * rows : (k + 1) * rows] = as_bf16(entry == cols[k : k + 1, :])
    before = as_bf16(
        lax.broadcasted_iota(jnp.int32, (rows, rows), 0) < lax.broadcasted_iota(jnp.int32, (rows, rows), 1)
    )
    mine = dall[me]
    sent = lax.broadcasted_iota(jnp.int32, (n, rows), 0) == jnp.right_shift(mine, shift)
    rank = dot(as_bf16(sent), before)
    for r in range(2):
        ohm[r] = as_bf16(sent & (rank == r))
    c_smat.wait()

    @pl.loop(0, smat.shape[0])
    def _(q):
        hi, lo = halves(smat[q])
        s_hi[q] = hi
        s_lo[q] = lo

    bytes_wait(dall.at[pl.ds(0, n - g1)], rs.at[3])
    dest = dall[:, 0, :]
    wanted = jnp.right_shift(dest, shift) == me
    slot = jnp.bitwise_and(dest, rows - 1).astype(F32)
    order = dot(as_bf16(wanted), before)
    lane = lax.broadcasted_iota(jnp.int32, (n, rows), 1).astype(F32)
    own = []
    for r in range(2):
        held = jnp.sum(jnp.where(wanted & (order == r), slot + 1.0, 0.0), axis=1, keepdims=True)
        own.append(as_bf16(lane + 1.0 == held))

    def ghosts(ghost, at):
        for side, there in ((0, dom > 0), (1, dom < nd - 1)):

            @pl.when(there)
            def _():
                bytes_wait(ghost.at[side], rs.at[at + side])

            @pl.when(jnp.logical_not(there))
            def _():
                ghost[side] = jnp.zeros(ghost.shape[1:], BF16)

    def gather(grp, ghost, near):
        total = None
        for b in range(nb):
            part = dot(grp[b], nearhot[b * rows : (b + 1) * rows, :])
            total = part if total is None else total + part
        for side in range(2):
            first = nb * rows + side * gmax
            total = total + dot(ghost[side], nearhot[first : first + gmax, :])
        for k in range(kblk):
            near[k] = total[:, k * rows : (k + 1) * rows]

    ghosts(ghost_d, 4)
    gather(grp_d, ghost_d, near_d)
    c_lap.wait()
    block_rows(lap, near_d, diffuse)

    fields = jnp.concatenate([disp[...], diffuse[...], dmg[...]], axis=0)
    f_hi, f_lo = halves(fields)
    for r in range(2):
        h2s[:, 0, r * wl : r * wl + 3 * width] = dot_nt(own[r], f_hi) + dot_nt(own[r], f_lo)

    def exchange(src, dst, at):
        pltpu.make_async_copy(src.at[me], dst.at[me], rs.at[at]).start()

        @pl.loop(0, n)
        def _(j):
            p = lax.rem(me + n // 2 + j, n)

            @pl.when(j != n // 2)
            def _():
                send(src.at[p], dst.at[me], ss.at[at], rs.at[at], p)

    exchange(h2s, h2r, 8)

    ghosts(ghost_w, 6)
    gather(grp_w, ghost_w, near_w)
    c_tan.wait()
    block_rows(tan, near_w, mech)
    c_load.wait()
    damage = dmg[...]
    root = jnp.sqrt((1.0 - damage) ** 2 + 0.001)
    mech_res = root * mech[...] - load[...]
    mech[...] = mech_res
    mech_part = jnp.sum(mech_res * mech_res)

    c_hist.wait()
    c_quad.wait()
    bytes_wait(h2r, rs.at[8])
    got = None
    for r in range(2):
        g_hi, g_lo = halves(jnp.transpose(h2r[:, 0, r * wl : r * wl + 3 * width]))
        part = dot(g_hi, ohm[r]) + dot(g_lo, ohm[r])
        got = part if got is None else got + part
    u_hi, u_lo = halves(got[:width])
    u_cat = jnp.concatenate([u_hi, u_lo], axis=1)

    def points(q, source):
        st = dot(s_hi[q], u_cat) + dot(s_lo[q], u_cat)
        st = st[:, :rows] + st[:, rows:]
        return source + quad[q] * jnp.maximum(hist[q], 0.5 * st * st)

    source = lax.fori_loop(0, smat.shape[0], points, jnp.zeros((width, rows), F32), unroll=3)
    there = got[2 * width :]
    dmg_res = got[width : 2 * width] + (1.0 + 2.0 * source) * there - 2.0 * source
    dmg_part = jnp.sum(dmg_res * dmg_res)

    pad = jnp.concatenate([dmg_res, jnp.zeros((LANES - width, rows), F32)], axis=0)
    p_hi, p_lo = halves(pad)
    lane = lax.broadcasted_iota(jnp.int32, (n, LANES), 1)
    for r in range(2):
        back = dot_nt(ohm[r], p_hi) + dot_nt(ohm[r], p_lo)
        if r == 0:
            back = jnp.where(lane == width, mech_part, jnp.where(lane == width + 1, dmg_part, back))
        h3s[:, 0, r * LANES : (r + 1) * LANES] = back
    exchange(h3s, h3r, 9)

    bytes_wait(h3r, rs.at[9])
    first = h3r[:, 0, :LANES]
    total = None
    for r in range(2):
        g_hi, g_lo = halves(jnp.transpose(h3r[:, 0, r * LANES : r * LANES + width]))
        part = dot(g_hi, own[r]) + dot(g_lo, own[r])
        total = part if total is None else total + part
    entries = n * rows * width
    sums = jnp.sum(first, axis=0, keepdims=True)
    norms = jnp.sqrt(sums * (1.0 / entries) + 1e-06)
    mech_o[...] = mech[...] / norms[:, width : width + 1]
    dmg_o[...] = total / norms[:, width + 1 : width + 2]
    norm_o[...] = norms

    bytes_wait(grp_d.at[pl.ds(0, nb - 1)], ss.at[0])
    bytes_wait(dall.at[pl.ds(0, g1 - 1)], ss.at[1])
    bytes_wait(grp_w.at[pl.ds(0, nb - 1)], ss.at[2])
    bytes_wait(dall.at[pl.ds(0, n - g1)], ss.at[3])
    for at, ghost in ((4, ghost_d), (6, ghost_w)):

        @pl.when(dom > 0)
        def _():
            bytes_wait(ghost.at[0], ss.at[at])

        @pl.when(dom < nd - 1)
        def _():
            bytes_wait(ghost.at[1], ss.at[at + 1])

    bytes_wait(h2s.at[pl.ds(0, n - 1)], ss.at[8])
    bytes_wait(h3s.at[pl.ds(0, n - 1)], ss.at[9])


def on_device(
    nd,
    nb,
    displacement,
    damage,
    applied_load,
    tangent,
    laplacian,
    block_columns,
    send_lists,
    hist_mech,
    mech_dest,
    strain_matrix,
    quad_weight,
):
    n = nd * nb
    rows, width = displacement.shape
    kblk = block_columns.shape[1]
    points = hist_mech.shape[1]
    gmax = send_lists.shape[2]
    wl = -(-3 * width // LANES) * LANES
    args = (
        displacement.T,
        damage.T,
        applied_load.T,
        jnp.transpose(tangent, (1, 2, 3, 0)),
        jnp.transpose(laplacian, (1, 2, 3, 0)),
        block_columns.T,
        send_lists[0],
        jnp.transpose(hist_mech, (1, 2, 0)),
        mech_dest.reshape(1, rows),
        strain_matrix,
        quad_weight,
    )
    vmem = pltpu.VMEM
    mech_out, dmg_out, norms = pl.pallas_call(
        functools.partial(kernel, nd, nb),
        out_shape=(
            jax.ShapeDtypeStruct((width, rows), F32),
            jax.ShapeDtypeStruct((width, rows), F32),
            jax.ShapeDtypeStruct((1, LANES), F32),
        ),
        in_specs=[pl.BlockSpec(memory_space=pl.ANY)] * len(args),
        out_specs=[pl.BlockSpec(memory_space=vmem)] * 3,
        scratch_shapes=[
            vmem((width, rows), F32),
            vmem((width, rows), F32),
            vmem((width, rows), F32),
            vmem((kblk, width, width, rows), BF16),
            vmem((kblk, width, width, rows), BF16),
            vmem((kblk, rows), jnp.int32),
            vmem((2, gmax), jnp.int32),
            vmem((points, width, rows), F32),
            vmem((points, width, width), F32),
            pltpu.SMEM((points,), F32),
            vmem((n, 1, rows), jnp.int32),
            vmem((nb, width, rows), BF16),
            vmem((nb, width, rows), BF16),
            vmem((2, width, gmax), BF16),
            vmem((2, width, gmax), BF16),
            vmem((2, width, gmax), BF16),
            vmem((2, width, gmax), BF16),
            vmem((2, nb * rows, gmax), BF16),
            vmem((nb * rows + 2 * gmax, kblk * rows), BF16),
            vmem((kblk, width, rows), F32),
            vmem((kblk, width, rows), F32),
            vmem((points, width, width), BF16),
            vmem((points, width, width), BF16),
            vmem((width, rows), F32),
            vmem((width, rows), F32),
            vmem((2, n, rows), BF16),
            vmem((n, 1, 2 * wl), F32),
            vmem((n, 1, 2 * wl), F32),
            vmem((n, 1, 2 * LANES), F32),
            vmem((n, 1, 2 * LANES), F32),
            pltpu.SemaphoreType.DMA((11,)),
            pltpu.SemaphoreType.DMA((10,)),
            pltpu.SemaphoreType.DMA((10,)),
        ],
        compiler_params=pltpu.CompilerParams(
            collective_id=0, has_side_effects=True, vmem_limit_bytes=60 << 20
        ),
        name="fracture_pass",
    )(*args)
    return mech_out.T, dmg_out.T, norms[0, width : width + 2]


def solution(mesh):
    both = ("dom", "blk")
    in_specs = (
        P(both, None),
        P(both, None),
        P(both, None),
        P(both, None, None, None),
        P(both, None, None, None),
        P(both, None),
        P("dom", None, None),
        P(both, None, None),
        P(both),
        P(),
        P(),
    )
    return jax.shard_map(
        functools.partial(on_device, mesh.shape["dom"], mesh.shape["blk"]),
        mesh=mesh,
        in_specs=in_specs,
        out_specs=(P(both, None), P(both, None), P()),
        check_vma=False,
    )
```

time: 225 us -> 46.7 us (0.21)
  blocking collectives: 73.8 us -> 0 us
  local copies, waits for them, and re-layouts: 69.6 us -> 4.1 us
  Pallas kernels: 0 us -> 41.7 us
  waiting for transfers between devices: 27.7 us -> 0 us
  starting transfers between devices: 26.3 us -> 0 us
  other arithmetic: 19.6 us -> 0 us
  matrix products: 4.4 us -> 0 us
    psum x1 -> x0, blocking collectives: 62.7 us -> none  [on_device(): lax.psum((jnp.sum(mech_res * mech_res), jnp.sum(dmg_res * dmg_res)), ('do...]
    pallas_call x0 -> x1, Pallas kernels: none -> 41.7 us  [on_device(): pl.pallas_call(functools.partial(kernel, nd, nb), out_shape=(jax.ShapeDty...]
    scatter x4 -> x0, local copies, waits for them, and re-layouts: 40.7 us -> none  [the longest x2 24 us: on_device(): history = jnp.zeros_like(hist_mech).at[target].set(got_rows.reshape((-1,)...]
    all_to_all x2 -> x0, waiting for transfers between devices: 27.7 us -> none  [the longest x1 27.7 us: on_device(): lax.all_to_all(parcel, ('dom', 'blk'), split_axis=0, concat_axis=0, tiled...]
    all_to_all x2 -> x0, starting transfers between devices: 19.1 us -> none  [the longest x1 10.2 us: on_device(): lax.all_to_all(parcel, ('dom', 'blk'), split_axis=0, concat_axis=0, tiled...]
    reshape x2 -> x0, local copies, waits for them, and re-layouts: 11.4 us -> none  [the longest x1 7.42 us: on_device(): parcel = parcel.reshape((devices, capacity) + hist_mech.shape[1:])]
    dot_general x1 -> x0, other arithmetic: 11.1 us -> none  [on_device(): jnp.einsum('ikrc,ikc->ir', laplacian, near_rows[1], preferred_element_typ...]
    all_gather x1 -> x0, blocking collectives: 11.1 us -> none  [on_device(): group_fields = lax.all_gather(fields, 'blk', axis=1, tiled=True)]
  transfers between devices with their start and end apart: 4 -> 0, of which waited for: 1 -> 0; matrix products, arithmetic and copies ran while one was open for 21% -> 0% of each run, Pallas kernels for 0% -> 0%
where the time goes in v1:
time: 46.7 us; the launch traced here: 46.5 us
  Pallas kernels  41.7 us (89%)
  local copies, waits for them, and re-layouts  4.1 us (9%)
  between operations  0.64 us (1%)
    pallas_call x1, Pallas kernels, on_device(): pl.pallas_call(functools.partial(kernel, nd, nb), out_shape=(jax.ShapeDty...  41.7 us
    unnamed x2, local copies, waits for them, and re-layouts  2.84 us
    squeeze x1, local copies, waits for them, and re-layouts, on_device(): return (mech_out.T, dmg_out.T, norms[0, width:width + 2])  1.26 us

profile of v1, /device:TPU:1, one launch (start us, length us, event | category | flops | bytes accessed | tf_op | source)
XLA Modules:
  0.0 46.5 jit_solution(14623752008314605672)
XLA Ops:
  0.6 41.7 %fracture_pass.1 = (f32[96,128]{1,0:T(8,128)}, f32[96,128]{1,0:T(8,128)}, f32[1,128]{1,0:T(1,128)}) custom-call(f32[96,128]{1,0:T(8,128)} %bitcast.18, f32[96,128]{1,0:T(8,128)} %bitcast.19, f32[96,128]{1,0:T(8,128)} %bitcast.20, bf16[5,96,96,128]{3,2,1,0:T(8,128)(2,1)} %bitcast.13, bf16[5,96,96,128]{3,2,1,0:T(8,128)(2,1)} %bitcast.14, s32[5,128]{1,0:T(8,128)} %bitcast.21, ...), custom_call_target="tpu_custom_call" | custom-call | tf_op jit(solution)/shard_map/fracture_pass/pallas_call | solution.py:403
  42.4 1.3 %slice_bitcast_fusion = f32[2]{0:T(128)} fusion(f32[1,128]{1,0:T(1,128)} %get-tuple-element.8), kind=kLoop, calls=%fused_computation | loop fusion | bytes 16 | tf_op jit(solution)/shard_map/squeeze | solution.py:452
  43.6 1.4 %copy.16 = f32[128,96]{0,1:T(8,128)} copy(f32[128,96]{0,1:T(8,128)} %bitcast.17) | data formatting | bytes 98304
  45.1 1.4 %copy.17 = f32[128,96]{0,1:T(8,128)} copy(f32[128,96]{0,1:T(8,128)} %bitcast.16) | data formatting | bytes 98304

commit v2 on v1

--- a/solution.py
+++ b/solution.py
@@ -1,4 +1,5 @@
 import functools
+import math
 
 import jax
 import jax.numpy as jnp
@@ -108,11 +109,19 @@
     kblk = cols.shape[0]
     gmax = lists.shape[1]
     shift = rows.bit_length() - 1
-    wl = h2s.shape[2] // 2
     dom = lax.axis_index("dom")
     blk = lax.axis_index("blk")
     me = dom * nb + blk
     base = (me // g1) * g1
+
+    side = math.isqrt(g2)
+
+    def hops(up):
+        z, x = divmod(up, side)
+        return min(z, side - z) + min(x, side - x)
+
+    far_groups = sorted(range(g2), key=hops, reverse=True)
+    far_peers = range(g1 - 1, -1, -1)
 
     def loc(p):
         return (p // nb, lax.rem(p, nb))
@@ -168,14 +177,14 @@
     c_dest.wait()
     pl.semaphore_wait(barrier, g1 + g2)
 
+    @pl.loop(1, g1)
+    def _(j):
+        send(dall.at[me], dall.at[me], ss.at[1], rs.at[1], base + lax.rem(me + j, g1))
+
     @pl.loop(1, nb)
     def _(j):
         p = dom * nb + lax.rem(blk + j, nb)
         send(grp_d.at[blk], grp_d.at[blk], ss.at[0], rs.at[0], p)
-
-    @pl.loop(1, g1)
-    def _(j):
-        send(dall.at[me], dall.at[me], ss.at[1], rs.at[1], base + lax.rem(me + j, g1))
 
     @pl.loop(1, nb)
     def _(j):
@@ -235,6 +244,33 @@
         s_hi[q] = hi
         s_lo[q] = lo
 
+    def ghosts(ghost, at):
+        for side, there in ((0, dom > 0), (1, dom < nd - 1)):
+
+            @pl.when(there)
+            def _():
+                bytes_wait(ghost.at[side], rs.at[at + side])
+
+            @pl.when(jnp.logical_not(there))
+            def _():
+                ghost[side] = jnp.zeros(ghost.shape[1:], BF16)
+
+    def gather(grp, ghost, near):
+        total = None
+        for b in range(nb):
+            part = dot(grp[b], nearhot[b * rows : (b + 1) * rows, :])
+            total = part if total is None else total + part
+        for side in range(2):
+            first = nb * rows + side * gmax
+            total = total + dot(ghost[side], nearhot[first : first + gmax, :])
+        for k in range(kblk):
+            near[k] = total[:, k * rows : (k + 1) * rows]
+
+    ghosts(ghost_d, 4)
+    gather(grp_d, ghost_d, near_d)
+    c_lap.wait()
+    block_rows(lap, near_d, diffuse)
+
     bytes_wait(dall.at[pl.ds(0, n - g1)], rs.at[3])
     dest = dall[:, 0, :]
     wanted = jnp.right_shift(dest, shift) == me
@@ -246,48 +282,27 @@
         held = jnp.sum(jnp.where(wanted & (order == r), slot + 1.0, 0.0), axis=1, keepdims=True)
         own.append(as_bf16(lane + 1.0 == held))
 
-    def ghosts(ghost, at):
-        for side, there in ((0, dom > 0), (1, dom < nd - 1)):
-
-            @pl.when(there)
-            def _():
-                bytes_wait(ghost.at[side], rs.at[at + side])
-
-            @pl.when(jnp.logical_not(there))
-            def _():
-                ghost[side] = jnp.zeros(ghost.shape[1:], BF16)
-
-    def gather(grp, ghost, near):
-        total = None
-        for b in range(nb):
-            part = dot(grp[b], nearhot[b * rows : (b + 1) * rows, :])
-            total = part if total is None else total + part
-        for side in range(2):
-            first = nb * rows + side * gmax
-            total = total + dot(ghost[side], nearhot[first : first + gmax, :])
-        for k in range(kblk):
-            near[k] = total[:, k * rows : (k + 1) * rows]
-
-    ghosts(ghost_d, 4)
-    gather(grp_d, ghost_d, near_d)
-    c_lap.wait()
-    block_rows(lap, near_d, diffuse)
-
     fields = jnp.concatenate([disp[...], diffuse[...], dmg[...]], axis=0)
     f_hi, f_lo = halves(fields)
-    for r in range(2):
-        h2s[:, 0, r * wl : r * wl + 3 * width] = dot_nt(own[r], f_hi) + dot_nt(own[r], f_lo)
+    both = jnp.concatenate(own, axis=1)
+    void = jnp.zeros(f_hi.shape, BF16)
+
+    def twice(f):
+        top = jnp.concatenate([f, void], axis=1)
+        low = jnp.concatenate([void, f], axis=1)
+        return jnp.concatenate([top, low], axis=0)
+
+    h2s[:, 0, : 6 * width] = dot_nt(both, twice(f_hi)) + dot_nt(both, twice(f_lo))
 
     def exchange(src, dst, at):
         pltpu.make_async_copy(src.at[me], dst.at[me], rs.at[at]).start()
 
-        @pl.loop(0, n)
-        def _(j):
-            p = lax.rem(me + n // 2 + j, n)
-
-            @pl.when(j != n // 2)
-            def _():
-                send(src.at[p], dst.at[me], ss.at[at], rs.at[at], p)
+        for up in far_groups:
+            first = lax.rem(base + up * g1, n)
+            for low in far_peers:
+                if up or low:
+                    p = first + jnp.bitwise_xor(me - base, low)
+                    send(src.at[p], dst.at[me], ss.at[at], rs.at[at], p)
 
     exchange(h2s, h2r, 8)
 
@@ -305,10 +320,11 @@
     c_hist.wait()
     c_quad.wait()
     bytes_wait(h2r, rs.at[8])
+    g_hi, g_lo = halves(jnp.transpose(h2r[:, 0, : 6 * width]))
     got = None
     for r in range(2):
-        g_hi, g_lo = halves(jnp.transpose(h2r[:, 0, r * wl : r * wl + 3 * width]))
-        part = dot(g_hi, ohm[r]) + dot(g_lo, ohm[r])
+        rows_r = slice(r * 3 * width, (r + 1) * 3 * width)
+        part = dot(g_hi[rows_r], ohm[r]) + dot(g_lo[rows_r], ohm[r])
         got = part if got is None else got + part
     u_hi, u_lo = halves(got[:width])
     u_cat = jnp.concatenate([u_hi, u_lo], axis=1)
@@ -318,7 +334,7 @@
         st = st[:, :rows] + st[:, rows:]
         return source + quad[q] * jnp.maximum(hist[q], 0.5 * st * st)
 
-    source = lax.fori_loop(0, smat.shape[0], points, jnp.zeros((width, rows), F32), unroll=3)
+    source = lax.fori_loop(0, smat.shape[0], points, jnp.zeros((width, rows), F32), unroll=True)
     there = got[2 * width :]
     dmg_res = got[width : 2 * width] + (1.0 + 2.0 * source) * there - 2.0 * source
     dmg_part = jnp.sum(dmg_res * dmg_res)
@@ -343,9 +359,9 @@
     entries = n * rows * width
     sums = jnp.sum(first, axis=0, keepdims=True)
     norms = jnp.sqrt(sums * (1.0 / entries) + 1e-06)
-    mech_o[...] = mech[...] / norms[:, width : width + 1]
-    dmg_o[...] = total / norms[:, width + 1 : width + 2]
-    norm_o[...] = norms
+    mech_o[...] = mech[...]
+    dmg_o[...] = total
+    norm_o[...] = norms[:, width : width + 2]
 
     bytes_wait(grp_d.at[pl.ds(0, nb - 1)], ss.at[0])
     bytes_wait(dall.at[pl.ds(0, g1 - 1)], ss.at[1])
@@ -363,6 +379,13 @@
 
     bytes_wait(h2s.at[pl.ds(0, n - 1)], ss.at[8])
     bytes_wait(h3s.at[pl.ds(0, n - 1)], ss.at[9])
+
+
+def normalize(mech, dmg, norm, mech_o, dmg_o, norm_o):
+    norms = norm[...]
+    mech_o[...] = mech[...] / norms[:, 0:1]
+    dmg_o[...] = dmg[...] / norms[:, 1:2]
+    norm_o[...] = norms
 
 
 def on_device(
@@ -385,7 +408,7 @@
     kblk = block_columns.shape[1]
     points = hist_mech.shape[1]
     gmax = send_lists.shape[2]
-    wl = -(-3 * width // LANES) * LANES
+    wl = -(-6 * width // LANES) * LANES
     args = (
         displacement.T,
         damage.T,
@@ -400,12 +423,12 @@
         quad_weight,
     )
     vmem = pltpu.VMEM
-    mech_out, dmg_out, norms = pl.pallas_call(
+    residuals = pl.pallas_call(
         functools.partial(kernel, nd, nb),
         out_shape=(
             jax.ShapeDtypeStruct((width, rows), F32),
             jax.ShapeDtypeStruct((width, rows), F32),
-            jax.ShapeDtypeStruct((1, LANES), F32),
+            jax.ShapeDtypeStruct((1, 2), F32),
         ),
         in_specs=[pl.BlockSpec(memory_space=pl.ANY)] * len(args),
         out_specs=[pl.BlockSpec(memory_space=vmem)] * 3,
@@ -436,8 +459,8 @@
             vmem((width, rows), F32),
             vmem((width, rows), F32),
             vmem((2, n, rows), BF16),
-            vmem((n, 1, 2 * wl), F32),
-            vmem((n, 1, 2 * wl), F32),
+            vmem((n, 1, wl), F32),
+            vmem((n, 1, wl), F32),
             vmem((n, 1, 2 * LANES), F32),
             vmem((n, 1, 2 * LANES), F32),
             pltpu.SemaphoreType.DMA((11,)),
@@ -449,7 +472,16 @@
         ),
         name="fracture_pass",
     )(*args)
-    return mech_out.T, dmg_out.T, norms[0, width : width + 2]
+    mech_out, dmg_out, norms = pl.pallas_call(
+        normalize,
+        out_shape=(
+            jax.ShapeDtypeStruct((width, rows), F32),
+            jax.ShapeDtypeStruct((width, rows), F32),
+            jax.ShapeDtypeStruct((1, 2), F32),
+        ),
+        name="normalize",
+    )(*residuals)
+    return mech_out.T, dmg_out.T, norms.reshape(2)
 
 
 def solution(mesh):

time: 46.7 us -> 38.1 us (0.82)
  Pallas kernels: 41.7 us -> 37.3 us
  local copies, waits for them, and re-layouts: 4.1 us -> 0 us
    pallas_call x1, Pallas kernels: 41.7 us -> 35.8 us  [on_device(): pl.pallas_call(functools.partial(kernel, nd, nb), out_shape=(jax.ShapeDty...]
    unnamed x2 -> x0, local copies, waits for them, and re-layouts: 2.84 us -> none
    pallas_call x0 -> x1, Pallas kernels: none -> 1.55 us  [on_device(): pl.pallas_call(normalize, out_shape=(jax.ShapeDtypeStruct((width, rows),...]
    squeeze x1 -> x0, local copies, waits for them, and re-layouts: 1.26 us -> none  [on_device(): return (mech_out.T, dmg_out.T, norms[0, width:width + 2])]
where the time goes in v2:
time: 38.1 us; the launch traced here: 38 us
  Pallas kernels  37.3 us (98%)
  between operations  0.64 us (2%)
    pallas_call x1, Pallas kernels, on_device(): pl.pallas_call(functools.partial(kernel, nd, nb), out_shape=(jax.ShapeDty...  35.8 us
    pallas_call x1, Pallas kernels, on_device(): pl.pallas_call(normalize, out_shape=(jax.ShapeDtypeStruct((width, rows),...  1.55 us

profile of v2, /device:TPU:1, one launch (start us, length us, event | category | flops | bytes accessed | tf_op | source)
XLA Modules:
  0.0 38.0 jit_solution(7710150653423602282)
XLA Ops:
  0.6 35.8 %fracture_pass.1 = (f32[96,128]{1,0:T(8,128)}, f32[96,128]{1,0:T(8,128)}, f32[1,2]{1,0:T(1,128)}) custom-call(f32[96,128]{1,0:T(8,128)} %bitcast.15, f32[96,128]{1,0:T(8,128)} %bitcast.16, f32[96,128]{1,0:T(8,128)} %bitcast.17, bf16[5,96,96,128]{3,2,1,0:T(8,128)(2,1)} %bitcast.12, bf16[5,96,96,128]{3,2,1,0:T(8,128)(2,1)} %bitcast.13, s32[5,128]{1,0:T(8,128)} %bitcast.18, ...), custom_call_target="tpu_custom_call" | custom-call | tf_op jit(solution)/shard_map/fracture_pass/pallas_call | solution.py:426
  36.4 1.5 %normalize.1 = (f32[96,128]{1,0:T(8,128)}, f32[96,128]{1,0:T(8,128)}, f32[1,2]{1,0:T(1,128)}) custom-call(f32[96,128]{1,0:T(8,128)} %get-tuple-element.9.mech, f32[96,128]{1,0:T(8,128)} %get-tuple-element.10.dmg, f32[1,2]{1,0:T(1,128)} %get-tuple-element.11.norm), custom_call_target="tpu_custom_call" | custom-call | tf_op jit(solution)/shard_map/normalize/pallas_call | solution.py:475

commit v3 on v2

--- a/solution.py
+++ b/solution.py
@@ -89,8 +89,7 @@
     nearhot,
     near_d,
     near_w,
-    s_hi,
-    s_lo,
+    s_cat,
     diffuse,
     mech,
     ohm,
@@ -104,30 +103,37 @@
 ):
     n = nd * nb
     g1 = 2 * nb
-    g2 = n // g1
+    side = math.isqrt(n // g1)
     width, rows = disp.shape
     kblk = cols.shape[0]
     gmax = lists.shape[1]
     shift = rows.bit_length() - 1
     dom = lax.axis_index("dom")
     blk = lax.axis_index("blk")
+    core = lax.rem(dom, 2)
+    z, x = dom // (2 * side), lax.rem(dom // 2, side)
     me = dom * nb + blk
-    base = (me // g1) * g1
-
-    side = math.isqrt(g2)
-
-    def hops(up):
-        z, x = divmod(up, side)
-        return min(z, side - z) + min(x, side - x)
-
-    far_groups = sorted(range(g2), key=hops, reverse=True)
+    cy = core * nb + blk
+
+    def at(z, x, cy):
+        return (z * side + x) * g1 + cy
+
+    def turn(c, step):
+        return lax.rem(c + step, side)
+
+    def hops(zx):
+        return sum(min(c, side - c) for c in zx)
+
+    far_groups = sorted(((a, b) for a in range(side) for b in range(side)), key=hops, reverse=True)
     far_peers = range(g1 - 1, -1, -1)
+    peers_x = [at(z, turn(x, step), cy) for step in range(1, side)]
+    peers_z = [at(turn(z, step), x, cy) for step in range(1, side)]
+    peers_cy = [at(z, x, jnp.bitwise_xor(cy, step)) for step in range(1, g1)]
+    peers_y = [at(z, x, core * nb + lax.rem(blk + step, nb)) for step in range(1, nb)]
+    across = lax.rem(jnp.where(core == 0, dom + nd - 1, dom + 1), nd) * nb + blk
 
     def loc(p):
         return (p // nb, lax.rem(p, nb))
-
-    def signal(p):
-        pl.semaphore_signal(barrier, inc=1, device_id=loc(p), device_id_type=MESH)
 
     def send(src, dst, s, r, p):
         pltpu.make_async_remote_copy(
@@ -135,24 +141,16 @@
         ).start()
 
     barrier = pltpu.get_barrier_semaphore()
-
-    @pl.loop(1, g1)
-    def _(j):
-        signal(base + lax.rem(me + j, g1))
-
-    @pl.loop(1, g2)
-    def _(j):
-        signal(lax.rem(me + g1 * j, n))
-
-    signal(lax.rem(me + nb, n))
-    signal(lax.rem(me + n - nb, n))
+    greeted = [across, *peers_x, *peers_z, *peers_cy]
+    for p in greeted:
+        pl.semaphore_signal(barrier, inc=1, device_id=loc(p), device_id_type=MESH)
 
     loads = []
     for i, (src, dst) in enumerate(
         (
+            (dest_h, dall.at[z, x, cy]),
             (dmg_h, dmg),
             (disp_h, disp),
-            (dest_h, dall.at[me]),
             (lists_h, lists),
             (cols_h, cols),
             (lap_h, lap),
@@ -166,63 +164,51 @@
         copy = pltpu.make_async_copy(src, dst, ld.at[i])
         copy.start()
         loads.append(copy)
-    c_dmg, c_disp, c_dest, c_lists, c_cols, c_lap, c_smat, c_hist, c_tan, c_load, c_quad = loads
+    c_dest, c_dmg, c_disp, c_lists, c_cols, c_lap, c_smat, c_hist, c_tan, c_load, c_quad = loads
 
     c_dmg.wait()
     damage = dmg[...]
     grp_d[blk] = damage.astype(BF16)
+    c_dest.wait()
+    pl.semaphore_wait(barrier, len(greeted))
+
+    def spread(part, peers, i):
+        for p in peers:
+            send(part, part, ss.at[i], rs.at[i], p)
+
+    spread(dall.at[z, x, cy], peers_x, 0)
+    spread(grp_d.at[blk], peers_y, 1)
+
     c_disp.wait()
     root = jnp.sqrt((1.0 - damage) ** 2 + 0.001)
     grp_w[blk] = (root * disp[...]).astype(BF16)
-    c_dest.wait()
-    pl.semaphore_wait(barrier, g1 + g2)
-
-    @pl.loop(1, g1)
-    def _(j):
-        send(dall.at[me], dall.at[me], ss.at[1], rs.at[1], base + lax.rem(me + j, g1))
-
-    @pl.loop(1, nb)
-    def _(j):
-        p = dom * nb + lax.rem(blk + j, nb)
-        send(grp_d.at[blk], grp_d.at[blk], ss.at[0], rs.at[0], p)
-
-    @pl.loop(1, nb)
-    def _(j):
-        p = dom * nb + lax.rem(blk + j, nb)
-        send(grp_w.at[blk], grp_w.at[blk], ss.at[2], rs.at[2], p)
-
+    spread(grp_w.at[blk], peers_y, 3)
     c_lists.wait()
-    for side in range(2):
+    for which in range(2):
         row = lax.broadcasted_iota(jnp.int32, (nb * rows, gmax), 0)
-        pickhot[side] = as_bf16(row == lists[side : side + 1, :])
-
-    bytes_wait(dall.at[pl.ds(0, g1 - 1)], rs.at[1])
-
-    @pl.loop(1, g2)
-    def _(j):
-        part = dall.at[pl.ds(base, g1)]
-        send(part, part, ss.at[3], rs.at[3], lax.rem(me + g1 * j, n))
-
-    def pick(grp, out, ghost, at):
-        for side in range(2):
+        pickhot[which] = as_bf16(row == lists[which : which + 1, :])
+
+    bytes_wait(dall.at[0, pl.ds(0, side - 1), 0], rs.at[0])
+    spread(dall.at[z, :, cy], peers_z, 2)
+
+    def pick(grp, out, ghost, i):
+        for which in range(2):
             total = None
             for b in range(nb):
-                part = dot(grp[b], pickhot[side, b * rows : (b + 1) * rows, :])
+                part = dot(grp[b], pickhot[which, b * rows : (b + 1) * rows, :])
                 total = part if total is None else total + part
-            out[side] = total.astype(BF16)
+            out[which] = total.astype(BF16)
 
         @pl.when(dom > 0)
         def _():
-            send(out.at[0], ghost.at[1], ss.at[at], rs.at[at + 1], me - nb)
+            send(out.at[0], ghost.at[1], ss.at[i], rs.at[i + 1], me - nb)
 
         @pl.when(dom < nd - 1)
         def _():
-            send(out.at[1], ghost.at[0], ss.at[at + 1], rs.at[at], me + nb)
-
-    bytes_wait(grp_d.at[pl.ds(0, nb - 1)], rs.at[0])
+            send(out.at[1], ghost.at[0], ss.at[i + 1], rs.at[i], me + nb)
+
+    bytes_wait(grp_d.at[pl.ds(0, nb - 1)], rs.at[1])
     pick(grp_d, pick_d, ghost_d, 4)
-    bytes_wait(grp_w.at[pl.ds(0, nb - 1)], rs.at[2])
-    pick(grp_w, pick_w, ghost_w, 6)
 
     c_cols.wait()
     for k in range(kblk):
@@ -231,38 +217,37 @@
     before = as_bf16(
         lax.broadcasted_iota(jnp.int32, (rows, rows), 0) < lax.broadcasted_iota(jnp.int32, (rows, rows), 1)
     )
-    mine = dall[me]
+    mine = dall[z, x, cy]
     sent = lax.broadcasted_iota(jnp.int32, (n, rows), 0) == jnp.right_shift(mine, shift)
     rank = dot(as_bf16(sent), before)
     for r in range(2):
         ohm[r] = as_bf16(sent & (rank == r))
-    c_smat.wait()
-
-    @pl.loop(0, smat.shape[0])
-    def _(q):
-        hi, lo = halves(smat[q])
-        s_hi[q] = hi
-        s_lo[q] = lo
-
-    def ghosts(ghost, at):
-        for side, there in ((0, dom > 0), (1, dom < nd - 1)):
+
+    bytes_wait(grp_w.at[pl.ds(0, nb - 1)], rs.at[3])
+    pick(grp_w, pick_w, ghost_w, 6)
+
+    bytes_wait(dall.at[pl.ds(0, side - 1), :, 0], rs.at[2])
+    spread(dall.at[:, :, cy], peers_cy, 8)
+
+    def ghosts(ghost, i):
+        for which, there in ((0, dom > 0), (1, dom < nd - 1)):
 
             @pl.when(there)
             def _():
-                bytes_wait(ghost.at[side], rs.at[at + side])
+                bytes_wait(ghost.at[which], rs.at[i + which])
 
             @pl.when(jnp.logical_not(there))
             def _():
-                ghost[side] = jnp.zeros(ghost.shape[1:], BF16)
+                ghost[which] = jnp.zeros(ghost.shape[1:], BF16)
 
     def gather(grp, ghost, near):
         total = None
         for b in range(nb):
             part = dot(grp[b], nearhot[b * rows : (b + 1) * rows, :])
             total = part if total is None else total + part
-        for side in range(2):
-            first = nb * rows + side * gmax
-            total = total + dot(ghost[side], nearhot[first : first + gmax, :])
+        for which in range(2):
+            first = nb * rows + which * gmax
+            total = total + dot(ghost[which], nearhot[first : first + gmax, :])
         for k in range(kblk):
             near[k] = total[:, k * rows : (k + 1) * rows]
 
@@ -271,8 +256,8 @@
     c_lap.wait()
     block_rows(lap, near_d, diffuse)
 
-    bytes_wait(dall.at[pl.ds(0, n - g1)], rs.at[3])
-    dest = dall[:, 0, :]
+    bytes_wait(dall.at[:, :, pl.ds(0, g1 - 1)], rs.at[8])
+    dest = dall[:, :, :, 0, :].reshape(n, rows)
     wanted = jnp.right_shift(dest, shift) == me
     slot = jnp.bitwise_and(dest, rows - 1).astype(F32)
     order = dot(as_bf16(wanted), before)
@@ -294,17 +279,16 @@
 
     h2s[:, 0, : 6 * width] = dot_nt(both, twice(f_hi)) + dot_nt(both, twice(f_lo))
 
-    def exchange(src, dst, at):
-        pltpu.make_async_copy(src.at[me], dst.at[me], rs.at[at]).start()
-
-        for up in far_groups:
-            first = lax.rem(base + up * g1, n)
+    def exchange(src, dst, i):
+        pltpu.make_async_copy(src.at[me], dst.at[me], rs.at[i]).start()
+        for group in far_groups:
+            first = at(turn(z, group[0]), turn(x, group[1]), 0)
             for low in far_peers:
-                if up or low:
-                    p = first + jnp.bitwise_xor(me - base, low)
-                    send(src.at[p], dst.at[me], ss.at[at], rs.at[at], p)
-
-    exchange(h2s, h2r, 8)
+                if any(group) or low:
+                    p = first + jnp.bitwise_xor(cy, low)
+                    send(src.at[p], dst.at[me], ss.at[i], rs.at[i], p)
+
+    exchange(h2s, h2r, 9)
 
     ghosts(ghost_w, 6)
     gather(grp_w, ghost_w, near_w)
@@ -319,7 +303,15 @@
 
     c_hist.wait()
     c_quad.wait()
-    bytes_wait(h2r, rs.at[8])
+    c_smat.wait()
+
+    @pl.loop(0, smat.shape[0])
+    def _(q):
+        hi, lo = halves(smat[q])
+        gap = jnp.zeros((width, LANES - width), BF16)
+        s_cat[q] = jnp.concatenate([hi, gap, lo, gap], axis=1)
+
+    bytes_wait(h2r, rs.at[9])
     g_hi, g_lo = halves(jnp.transpose(h2r[:, 0, : 6 * width]))
     got = None
     for r in range(2):
@@ -328,9 +320,11 @@
         got = part if got is None else got + part
     u_hi, u_lo = halves(got[:width])
     u_cat = jnp.concatenate([u_hi, u_lo], axis=1)
+    gap = jnp.zeros((LANES - width, 2 * rows), BF16)
+    u_cat = jnp.concatenate([u_cat, gap, u_cat, gap], axis=0)
 
     def points(q, source):
-        st = dot(s_hi[q], u_cat) + dot(s_lo[q], u_cat)
+        st = dot(s_cat[q], u_cat)
         st = st[:, :rows] + st[:, rows:]
         return source + quad[q] * jnp.maximum(hist[q], 0.5 * st * st)
 
@@ -347,9 +341,9 @@
         if r == 0:
             back = jnp.where(lane == width, mech_part, jnp.where(lane == width + 1, dmg_part, back))
         h3s[:, 0, r * LANES : (r + 1) * LANES] = back
-    exchange(h3s, h3r, 9)
-
-    bytes_wait(h3r, rs.at[9])
+    exchange(h3s, h3r, 10)
+
+    bytes_wait(h3r, rs.at[10])
     first = h3r[:, 0, :LANES]
     total = None
     for r in range(2):
@@ -363,22 +357,23 @@
     dmg_o[...] = total
     norm_o[...] = norms[:, width : width + 2]
 
-    bytes_wait(grp_d.at[pl.ds(0, nb - 1)], ss.at[0])
-    bytes_wait(dall.at[pl.ds(0, g1 - 1)], ss.at[1])
-    bytes_wait(grp_w.at[pl.ds(0, nb - 1)], ss.at[2])
-    bytes_wait(dall.at[pl.ds(0, n - g1)], ss.at[3])
-    for at, ghost in ((4, ghost_d), (6, ghost_w)):
+    bytes_wait(dall.at[0, pl.ds(0, side - 1), 0], ss.at[0])
+    bytes_wait(grp_d.at[pl.ds(0, nb - 1)], ss.at[1])
+    bytes_wait(dall.at[pl.ds(0, side - 1), :, 0], ss.at[2])
+    bytes_wait(grp_w.at[pl.ds(0, nb - 1)], ss.at[3])
+    for i, ghost in ((4, ghost_d), (6, ghost_w)):
 
         @pl.when(dom > 0)
         def _():
-            bytes_wait(ghost.at[0], ss.at[at])
+            bytes_wait(ghost.at[0], ss.at[i])
 
         @pl.when(dom < nd - 1)
         def _():
-            bytes_wait(ghost.at[1], ss.at[at + 1])
-
-    bytes_wait(h2s.at[pl.ds(0, n - 1)], ss.at[8])
-    bytes_wait(h3s.at[pl.ds(0, n - 1)], ss.at[9])
+            bytes_wait(ghost.at[1], ss.at[i + 1])
+
+    bytes_wait(dall.at[:, :, pl.ds(0, g1 - 1)], ss.at[8])
+    bytes_wait(h2s.at[pl.ds(0, n - 1)], ss.at[9])
+    bytes_wait(h3s.at[pl.ds(0, n - 1)], ss.at[10])
 
 
 def normalize(mech, dmg, norm, mech_o, dmg_o, norm_o):
@@ -409,6 +404,7 @@
     points = hist_mech.shape[1]
     gmax = send_lists.shape[2]
     wl = -(-6 * width // LANES) * LANES
+    side = math.isqrt(nd // 2)
     args = (
         displacement.T,
         damage.T,
@@ -425,11 +421,7 @@
     vmem = pltpu.VMEM
     residuals = pl.pallas_call(
         functools.partial(kernel, nd, nb),
-        out_shape=(
-            jax.ShapeDtypeStruct((width, rows), F32),
-            jax.ShapeDtypeStruct((width, rows), F32),
-            jax.ShapeDtypeStruct((1, 2), F32),
-        ),
+        out_shape=(vmem((width, rows), F32), vmem((width, rows), F32), vmem((1, 2), F32)),
         in_specs=[pl.BlockSpec(memory_space=pl.ANY)] * len(args),
         out_specs=[pl.BlockSpec(memory_space=vmem)] * 3,
         scratch_shapes=[
@@ -443,7 +435,7 @@
             vmem((points, width, rows), F32),
             vmem((points, width, width), F32),
             pltpu.SMEM((points,), F32),
-            vmem((n, 1, rows), jnp.int32),
+            vmem((side, side, 2 * nb, 1, rows), jnp.int32),
             vmem((nb, width, rows), BF16),
             vmem((nb, width, rows), BF16),
             vmem((2, width, gmax), BF16),
@@ -454,8 +446,7 @@
             vmem((nb * rows + 2 * gmax, kblk * rows), BF16),
             vmem((kblk, width, rows), F32),
             vmem((kblk, width, rows), F32),
-            vmem((points, width, width), BF16),
-            vmem((points, width, width), BF16),
+            vmem((points, width, 2 * LANES), BF16),
             vmem((width, rows), F32),
             vmem((width, rows), F32),
             vmem((2, n, rows), BF16),
@@ -464,8 +455,8 @@
             vmem((n, 1, 2 * LANES), F32),
             vmem((n, 1, 2 * LANES), F32),
             pltpu.SemaphoreType.DMA((11,)),
-            pltpu.SemaphoreType.DMA((10,)),
-            pltpu.SemaphoreType.DMA((10,)),
+            pltpu.SemaphoreType.DMA((11,)),
+            pltpu.SemaphoreType.DMA((11,)),
         ],
         compiler_params=pltpu.CompilerParams(
             collective_id=0, has_side_effects=True, vmem_limit_bytes=60 << 20
@@ -479,8 +470,9 @@
             jax.ShapeDtypeStruct((width, rows), F32),
             jax.ShapeDtypeStruct((1, 2), F32),
         ),
+        in_specs=[pl.BlockSpec(memory_space=vmem)] * 3,
         name="normalize",
-    )(*residuals)
+    )(*(pltpu.with_memory_space_constraint(x, vmem) for x in residuals))
     return mech_out.T, dmg_out.T, norms.reshape(2)
 
 

time: 38.1 us -> 35.8 us (0.940)
  Pallas kernels: 37.3 us -> 35 us
    pallas_call x1, Pallas kernels: 35.8 us -> 34.3 us  [on_device(): pl.pallas_call(functools.partial(kernel, nd, nb), out_shape=(vmem((width,...]
    pallas_call x1, Pallas kernels: 1.55 us -> 0.72 us  [on_device(): pl.pallas_call(normalize, out_shape=(jax.ShapeDtypeStruct((width, rows),...]
where the time goes in v3:
time: 35.8 us; the launch traced here: 35.6 us
  Pallas kernels  35 us (98%)
  between operations  0.64 us (2%)
    pallas_call x1, Pallas kernels, on_device(): pl.pallas_call(functools.partial(kernel, nd, nb), out_shape=(vmem((width,...  34.3 us
    pallas_call x1, Pallas kernels, on_device(): pl.pallas_call(normalize, out_shape=(jax.ShapeDtypeStruct((width, rows),...  0.72 us

profile of v3, /device:TPU:1, one launch (start us, length us, event | category | flops | bytes accessed | tf_op | source)
XLA Modules:
  0.0 35.6 jit_solution(18114774024608284660)
XLA Ops:
  0.6 34.3 %fracture_pass.1 = (f32[96,128]{1,0:T(8,128)S(1)}, f32[96,128]{1,0:T(8,128)S(1)}, f32[1,2]{1,0:T(1,128)S(1)}) custom-call(f32[96,128]{1,0:T(8,128)} %bitcast.15, f32[96,128]{1,0:T(8,128)} %bitcast.16, f32[96,128]{1,0:T(8,128)} %bitcast.17, bf16[5,96,96,128]{3,2,1,0:T(8,128)(2,1)} %bitcast.12, bf16[5,96,96,128]{3,2,1,0:T(8,128)(2,1)} %bitcast.13, ...), custom_call_target="tpu_custom_call" | custom-call | tf_op jit(solution)/shard_map/fracture_pass/pallas_call | solution.py:422
  34.9 0.7 %normalize.1 = (f32[96,128]{1,0:T(8,128)}, f32[96,128]{1,0:T(8,128)}, f32[1,2]{1,0:T(1,128)}) custom-call(f32[96,128]{1,0:T(8,128)S(1)} %get-tuple-element.9.mech, f32[96,128]{1,0:T(8,128)S(1)} %get-tuple-element.10.dmg, f32[1,2]{1,0:T(1,128)S(1)} %get-tuple-element.11.norm), custom_call_target="tpu_custom_call" | custom-call | tf_op jit(solution)/shard_map/normalize/pallas_call | solution.py:466

commit v4 on v3

--- a/solution.py
+++ b/solution.py
@@ -36,19 +36,20 @@
 
 
 def block_rows(mat, near, out):
-    kblk, width = near.shape[0], near.shape[1]
-
-    def rows(rb, carry):
+    kblk, width = mat.shape[:2]
+
+    def eight(rb, carry):
         r0 = pl.multiple_of(rb * 8, 8)
         acc = None
         for k in range(kblk):
             for c in range(0, width, 16):
-                part = mat[k, pl.ds(r0, 8), c : c + 16, :].astype(F32) * near[k, c : c + 16, :][None]
+                first = k * width + c
+                part = mat[k, pl.ds(r0, 8), c : c + 16, :].astype(F32) * near[first : first + 16, :][None]
                 acc = part if acc is None else acc + part
         out[pl.ds(r0, 8), :] = jnp.sum(acc, axis=1)
         return carry
 
-    lax.fori_loop(0, width // 8, rows, 0)
+    lax.fori_loop(0, width // 8, eight, 0)
 
 
 def kernel(
@@ -140,11 +141,7 @@
             src_ref=src, dst_ref=dst, send_sem=s, recv_sem=r, device_id=loc(p), device_id_type=MESH
         ).start()
 
-    barrier = pltpu.get_barrier_semaphore()
     greeted = [across, *peers_x, *peers_z, *peers_cy]
-    for p in greeted:
-        pl.semaphore_signal(barrier, inc=1, device_id=loc(p), device_id_type=MESH)
-
     loads = []
     for i, (src, dst) in enumerate(
         (
@@ -164,6 +161,10 @@
         copy = pltpu.make_async_copy(src, dst, ld.at[i])
         copy.start()
         loads.append(copy)
+        if i == 1:
+            barrier = pltpu.get_barrier_semaphore()
+            for p in greeted:
+                pl.semaphore_signal(barrier, inc=1, device_id=loc(p), device_id_type=MESH)
     c_dest, c_dmg, c_disp, c_lists, c_cols, c_lap, c_smat, c_hist, c_tan, c_load, c_quad = loads
 
     c_dmg.wait()
@@ -209,6 +210,14 @@
 
     bytes_wait(grp_d.at[pl.ds(0, nb - 1)], rs.at[1])
     pick(grp_d, pick_d, ghost_d, 4)
+
+    def near_own(grp, near):
+        total = None
+        for b in range(nb):
+            part = dot(grp[b], nearhot[b * rows : (b + 1) * rows, :])
+            total = part if total is None else total + part
+        for k in range(kblk):
+            near[k * width : (k + 1) * width, :] = total[:, k * rows : (k + 1) * rows]
 
     c_cols.wait()
     for k in range(kblk):
@@ -223,6 +232,7 @@
     for r in range(2):
         ohm[r] = as_bf16(sent & (rank == r))
 
+    near_own(grp_d, near_d)
     bytes_wait(grp_w.at[pl.ds(0, nb - 1)], rs.at[3])
     pick(grp_w, pick_w, ghost_w, 6)
 
@@ -240,19 +250,17 @@
             def _():
                 ghost[which] = jnp.zeros(ghost.shape[1:], BF16)
 
-    def gather(grp, ghost, near):
+    def near_ghosts(ghost, near):
         total = None
-        for b in range(nb):
-            part = dot(grp[b], nearhot[b * rows : (b + 1) * rows, :])
-            total = part if total is None else total + part
         for which in range(2):
             first = nb * rows + which * gmax
-            total = total + dot(ghost[which], nearhot[first : first + gmax, :])
+            part = dot(ghost[which], nearhot[first : first + gmax, :])
+            total = part if total is None else total + part
         for k in range(kblk):
-            near[k] = total[:, k * rows : (k + 1) * rows]
+            near[k * width : (k + 1) * width, :] += total[:, k * rows : (k + 1) * rows]
 
     ghosts(ghost_d, 4)
-    gather(grp_d, ghost_d, near_d)
+    near_ghosts(ghost_d, near_d)
     c_lap.wait()
     block_rows(lap, near_d, diffuse)
 
@@ -290,8 +298,9 @@
 
     exchange(h2s, h2r, 9)
 
+    near_own(grp_w, near_w)
     ghosts(ghost_w, 6)
-    gather(grp_w, ghost_w, near_w)
+    near_ghosts(ghost_w, near_w)
     c_tan.wait()
     block_rows(tan, near_w, mech)
     c_load.wait()
@@ -444,8 +453,8 @@
             vmem((2, width, gmax), BF16),
             vmem((2, nb * rows, gmax), BF16),
             vmem((nb * rows + 2 * gmax, kblk * rows), BF16),
-            vmem((kblk, width, rows), F32),
-            vmem((kblk, width, rows), F32),
+            vmem((kblk * width, rows), F32),
+            vmem((kblk * width, rows), F32),
             vmem((points, width, 2 * LANES), BF16),
             vmem((width, rows), F32),
             vmem((width, rows), F32),

time: 35.8 us -> 35.7 us (level)
  no operation moved by 1% of the time
where the time goes in v4:
time: 35.7 us; the launch traced here: 35.6 us
  Pallas kernels  35 us (98%)
  between operations  0.64 us (2%)
    pallas_call x1, Pallas kernels, on_device(): pl.pallas_call(functools.partial(kernel, nd, nb), out_shape=(vmem((width,...  34.2 us
    pallas_call x1, Pallas kernels, on_device(): pl.pallas_call(normalize, out_shape=(jax.ShapeDtypeStruct((width, rows),...  0.72 us

profile of v4, /device:TPU:1, one launch (start us, length us, event | category | flops | bytes accessed | tf_op | source)
XLA Modules:
  0.0 35.6 jit_solution(1733049287559590643)
XLA Ops:
  0.6 34.2 %fracture_pass.1 = (f32[96,128]{1,0:T(8,128)S(1)}, f32[96,128]{1,0:T(8,128)S(1)}, f32[1,2]{1,0:T(1,128)S(1)}) custom-call(f32[96,128]{1,0:T(8,128)} %bitcast.15, f32[96,128]{1,0:T(8,128)} %bitcast.16, f32[96,128]{1,0:T(8,128)} %bitcast.17, bf16[5,96,96,128]{3,2,1,0:T(8,128)(2,1)} %bitcast.12, bf16[5,96,96,128]{3,2,1,0:T(8,128)(2,1)} %bitcast.13, ...), custom_call_target="tpu_custom_call" | custom-call | tf_op jit(solution)/shard_map/fracture_pass/pallas_call | solution.py:431
  34.9 0.7 %normalize.1 = (f32[96,128]{1,0:T(8,128)}, f32[96,128]{1,0:T(8,128)}, f32[1,2]{1,0:T(1,128)}) custom-call(f32[96,128]{1,0:T(8,128)S(1)} %get-tuple-element.9.mech, f32[96,128]{1,0:T(8,128)S(1)} %get-tuple-element.10.dmg, f32[1,2]{1,0:T(1,128)S(1)} %get-tuple-element.11.norm), custom_call_target="tpu_custom_call" | custom-call | tf_op jit(solution)/shard_map/normalize/pallas_call | solution.py:475
